TPU v7x, 256 devices: a whole 4x4x8 slice. The times are simulated.
256 devices in a mesh: dp: 32 (over z, y_hi, core), expert: 8 (over x, y_lo).
Axes of the slice: x: 4, y: 4 (y_hi: 2, y_lo: 2; y = y_hi * 2 + y_lo), z: 8, core: 2. Of those that a mesh axis runs over, the one named last changes fastest.
Arguments:
- tokens: bfloat16 [32768, 2048], P(('dp', 'expert')), may hold values from -24 to 24
- cotangent: bfloat16 [32768, 2048], P(('dp', 'expert')), may hold values from -24 to 24
- expert_ids: int32 [32768, 2], P(('dp', 'expert')), may hold values from 0 to 7, all different within a row; in each aligned block of 128 rows (0 to 127, 128 to 255, ...) at most 40 rows name the same one
- gate_weights: float32 [32768, 2], P(('dp', 'expert')), may hold values from 0.1 to 1
- partner: int32 [8], replicated, may hold values from 0 to 7, as said below
- w_gate: bfloat16 [8, 2048, 768], P('expert'), may hold values from -0.125 to 0.125
- w_up: bfloat16 [8, 2048, 768], P('expert'), may hold values from -0.125 to 0.125
- w_down: bfloat16 [8, 768, 2048], P('expert'), may hold values from -0.21875 to 0.21875
Outputs:
- mixed_out: bfloat16 [32768, 2048], P(('dp', 'expert'))
- token_grad: bfloat16 [32768, 2048], P(('dp', 'expert'))
- gate_grad: float32 [32768, 2], P(('dp', 'expert'))
- slot_grad_gate: float32 [8, 2048, 768], P('expert', 'dp')
- slot_grad_up: float32 [8, 2048, 768], P('expert', 'dp')
- slot_grad_down: float32 [8, 768, 2048], P('expert', None, 'dp')
Inputs may be any that keep to these rules, and one draw needn't show every extreme that they name: `expert_ids`: each row names 2 different experts. Among the 128 rows of one device no expert is named by more than 40 rows, and in every draw some device names some expert exactly 40 times. partner[partner[i]] = i and partner[i] != i for every slot i.
All inputs are finite; a program needn't handle non-finite values.
Results may differ from a plain program's by a relative error of at most 0.015.
Values may be sent and summed in bfloat16 or wider, within the bound.
A program may use at most 128 MiB of HBM per device.

v0:
```python
import jax
import jax.numpy as jnp
from jax import lax
from jax.sharding import PartitionSpec as P


def as_sent(shard):

    def short(part):
        return part.astype(jnp.bfloat16) if part.dtype == jnp.float32 else part

    return jax.tree.map(short, shard)


def contract_rows(left_mat, right_mat):
    return lax.dot_general(
        left_mat, right_mat, (((0,), (0,)), ((), ())), preferred_element_type=jnp.float32
    )


def contract_cols(left_mat, right_mat):
    return lax.dot_general(
        left_mat, right_mat, (((1,), (1,)), ((), ())), preferred_element_type=jnp.float32
    )


def pick_from(stacked, source):
    return lax.dynamic_index_in_dim(stacked, source, 0, keepdims=False)


def shards(tokens, cotangent, expert_ids, gate_weights, partner, w_gate, w_up, w_down):
    groups = lax.axis_size("expert")
    my_group = lax.axis_index("expert")
    tok_count, model_width = tokens.shape
    top_count = expert_ids.shape[1]
    capacity = min(tok_count, 5 * tok_count * top_count // (4 * groups))
    buffer_rows = groups * capacity
    group_ids = jnp.arange(groups, dtype=jnp.int32)
    my_mate = pick_from(partner, my_group)
    flat_ids = expert_ids.reshape(-1)
    dest_group = jnp.sum(
        jnp.where(flat_ids[:, None] == group_ids[None, :], partner[None, :], 0), axis=1
    )
    one_hot = (dest_group[:, None] == group_ids[None, :]).astype(jnp.int32)
    earlier = jnp.cumsum(one_hot, axis=0) - one_hot
    slot_index = dest_group * capacity + jnp.sum(earlier * one_hot, axis=1)
    place_mat = (slot_index[None, :] == jnp.arange(buffer_rows, dtype=jnp.int32)[:, None]).astype(
        jnp.bfloat16
    )
    replicas = lax.axis_size("dp")
    share_rows = model_width // replicas
    share_start = lax.axis_index("dp") * share_rows
    shares = (
        lax.dynamic_slice_in_dim(w_gate[0], share_start, share_rows, 0),
        lax.dynamic_slice_in_dim(w_up[0], share_start, share_rows, 0),
        lax.dynamic_slice_in_dim(w_down[0], share_start, share_rows, 1),
    )
    is_mate = (partner == my_group)[:, None, None]
    outgoing = tuple(
        (
            jnp.where(is_mate, own_share[None], jnp.zeros_like(own_share)[None])
            for own_share in shares
        )
    )
    incoming = jax.tree.map(
        lambda part, own: part.astype(own.dtype),
        lax.all_to_all(as_sent(outgoing), "expert", split_axis=0, concat_axis=0, tiled=True),
        outgoing,
    )
    mate_shares = tuple((pick_from(block_piece, my_mate) for block_piece in incoming))
    gate_mat, up_mat, down_mat = (
        lax.all_gather(mate_shares[0], "dp", axis=0, tiled=True),
        lax.all_gather(mate_shares[1], "dp", axis=0, tiled=True),
        lax.all_gather(mate_shares[2], "dp", axis=1, tiled=True),
    )
    repeated = jnp.repeat(tokens, top_count, axis=0)
    outgoing_rows = jnp.dot(place_mat, repeated, preferred_element_type=jnp.float32).astype(
        jnp.bfloat16
    )
    expert_in = lax.all_to_all(
        outgoing_rows.reshape(groups, capacity, model_width),
        "expert",
        split_axis=0,
        concat_axis=0,
        tiled=True,
    ).reshape(buffer_rows, model_width)
    gate_pre = jnp.dot(expert_in, gate_mat, preferred_element_type=jnp.float32)
    up_pre = jnp.dot(expert_in, up_mat, preferred_element_type=jnp.float32)
    sigmoid_gate = jax.nn.sigmoid(gate_pre)
    hidden = (gate_pre * sigmoid_gate * up_pre).astype(jnp.bfloat16)
    expert_out = jnp.dot(hidden, down_mat, preferred_element_type=jnp.float32).astype(jnp.bfloat16)
    returned = lax.all_to_all(
        expert_out.reshape(groups, capacity, model_width),
        "expert",
        split_axis=0,
        concat_axis=0,
        tiled=True,
    ).reshape(buffer_rows, model_width)
    per_assign = (
        jnp.take(returned, slot_index, axis=0)
        .astype(jnp.float32)
        .reshape(tok_count, top_count, model_width)
    )
    mixed_out = jnp.sum(gate_weights[:, :, None] * per_assign, axis=1).astype(jnp.bfloat16)
    cot_float = cotangent.astype(jnp.float32)
    gate_grad = jnp.sum(cot_float[:, None, :] * per_assign, axis=2)
    scaled = (
        (gate_weights[:, :, None] * cot_float[:, None, :])
        .astype(jnp.bfloat16)
        .reshape(-1, model_width)
    )
    outgoing_grads = jnp.dot(place_mat, scaled, preferred_element_type=jnp.float32).astype(
        jnp.bfloat16
    )
    grads_in = lax.all_to_all(
        outgoing_grads.reshape(groups, capacity, model_width),
        "expert",
        split_axis=0,
        concat_axis=0,
        tiled=True,
    ).reshape(buffer_rows, model_width)
    hidden_grad = contract_cols(grads_in, down_mat)
    gate_grad_pre = (
        hidden_grad * up_pre * sigmoid_gate * (1.0 + gate_pre * (1.0 - sigmoid_gate))
    ).astype(jnp.bfloat16)
    up_grad_pre = (hidden_grad * gate_pre * sigmoid_gate).astype(jnp.bfloat16)
    row_grad = (contract_cols(gate_grad_pre, gate_mat) + contract_cols(up_grad_pre, up_mat)).astype(
        jnp.bfloat16
    )
    returned_grads = lax.all_to_all(
        row_grad.reshape(groups, capacity, model_width),
        "expert",
        split_axis=0,
        concat_axis=0,
        tiled=True,
    ).reshape(buffer_rows, model_width)
    grad_rows = (
        jnp.take(returned_grads, slot_index, axis=0)
        .astype(jnp.float32)
        .reshape(tok_count, top_count, model_width)
    )
    token_grad = jnp.sum(grad_rows, axis=1).astype(jnp.bfloat16)
    partial_gate = contract_rows(expert_in, gate_grad_pre)
    partial_up = contract_rows(expert_in, up_grad_pre)
    partial_down = contract_rows(hidden, grads_in)
    sum_gate, sum_up, sum_down = (
        lax.psum_scatter(
            partial_gate.astype(jnp.bfloat16), "dp", scatter_dimension=0, tiled=True
        ).astype(jnp.float32),
        lax.psum_scatter(
            partial_up.astype(jnp.bfloat16), "dp", scatter_dimension=0, tiled=True
        ).astype(jnp.float32),
        lax.psum_scatter(
            partial_down.astype(jnp.bfloat16), "dp", scatter_dimension=1, tiled=True
        ).astype(jnp.float32),
    )
    return (mixed_out, token_grad, gate_grad, sum_gate[None], sum_up[None], sum_down[None])


def solution(mesh):
    in_specs = (
        P(("dp", "expert"), None),
        P(("dp", "expert"), None),
        P(("dp", "expert"), None),
        P(("dp", "expert"), None),
        P(),
        P("expert", None, None),
        P("expert", None, None),
        P("expert", None, None),
    )
    out_specs = (
        P(("dp", "expert"), None),
        P(("dp", "expert"), None),
        P(("dp", "expert"), None),
        P("expert", "dp", None),
        P("expert", "dp", None),
        P("expert", None, "dp"),
    )
    return jax.shard_map(shards, mesh=mesh, in_specs=in_specs, out_specs=out_specs, check_vma=False)
```

profile of v0, /device:TPU:4, one launch (start us, length us, event | category | flops | bytes accessed | tf_op | source)
XLA Modules:
  0.0 688.2 jit_solution(8233593337685913203)
XLA Ops:
  10.5 6.3 all-to-all-start.2
  19.3 7.3 %all-to-all-done.2 = bf16[8,64,768]{2,1,0:T(8,128)(2,1)} async-done(((bf16[8,64,768]{2,1,0:T(8,128)(2,1)}), bf16[8,64,768]{2,1,0:T(8,128)(2,1)}, u32[]{:S(2)}, u32[]{:S(2)}) %all-to-all-start.2) | async-done | bytes 786464 | tf_op jit(solution)/shard_map/all_to_all | solution.py:67
  28.7 15.4 %all_to_all.35 = bf16[8,768,64]{1,2,0:T(8,128)(2,1)S(1)} all-to-all(bf16[8,768,64]{1,2,0:T(8,128)(2,1)S(1)} %broadcast_select_fusion.1), channel_id=1, replica_groups=mesh['dp'=32,'expert'=8] {'expert'}, dimensions={0} | all-to-all | bytes 1572864 | tf_op jit(solution)/shard_map/all_to_all | solution.py:67
  44.8 13.8 %all_to_all.36 = bf16[8,64,768]{2,1,0:T(8,128)(2,1)S(1)} all-to-all(bf16[8,64,768]{2,1,0:T(8,128)(2,1)S(1)} %copy-done.6), channel_id=1, replica_groups=mesh['dp'=32,'expert'=8] {'expert'}, dimensions={0} | all-to-all | bytes 1572864 | tf_op jit(solution)/shard_map/all_to_all | solution.py:67
  63.2 6.2 all-to-all-start
  69.5 2.4 mul.83
  71.9 2.7 mul.84
  76.5 6.3 all-to-all-done
  82.8 7.1 %all-to-all-start.5 = ((bf16[8,40,2048]{2,1,0:T(8,128)(2,1)}), bf16[8,40,2048]{2,1,0:T(8,128)(2,1)}, u32[]{:S(2)}, u32[]{:S(2)}) async-start(bf16[8,40,2048]{2,1,0:T(8,128)(2,1)} %bitcast.70), calls=%async_computation.5 | async-start | bytes 2621440 | tf_op jit(solution)/shard_map/all_to_all | solution.py:115
  89.9 34.6 %all-gather.9.cloned.1.call-done = bf16[1,2048,768]{2,1,0:T(8,128)(2,1)} async-done(((bf16[1,64,768]{2,1,0:T(8,128)(2,1)}), bf16[1,2048,768]{2,1,0:T(8,128)(2,1)}) %all-gather.9.cloned.1.call-update) | async-done | bytes 3145744 | tf_op jit(solution)/shard_map/all_gather | solution.py:73
  124.5 3.5 fusion.6
  128.0 79.0 %all-gather.11.cloned.1.call-done = bf16[1,768,2048]{1,2,0:T(8,128)(2,1)} async-done(((bf16[1,768,64]{1,2,0:T(8,128)(2,1)}), bf16[1,768,2048]{1,2,0:T(8,128)(2,1)}) %all-gather.11.cloned.1.call-update) | async-done | bytes 3145744 | tf_op jit(solution)/shard_map/all_gather | solution.py:74
  206.9 3.5 fusion
  210.4 79.6 %all-gather.7.cloned.1.call-done = bf16[1,2048,768]{2,1,0:T(8,128)(2,1)} async-done(((bf16[1,64,768]{2,1,0:T(8,128)(2,1)}), bf16[1,2048,768]{2,1,0:T(8,128)(2,1)}) %all-gather.7.cloned.1.call-update) | async-done | bytes 3145744 | tf_op jit(solution)/shard_map/all_gather | solution.py:72
  290.0 3.7 multiply_convert_fusion.3
  294.5 4.8 convolution_convert_fusion
  299.6 4.9 convolution_convert_fusion.1
  304.5 4.8 convolution_convert_fusion.2
  309.4 3.3 fusion.4
  315.1 5.0 all-to-all-start.6
  320.0 4.3 fusion.18
  324.3 12.7 %all-to-all-done.6 = bf16[8,40,2048]{2,1,0:T(8,128)(2,1)S(1)} async-done(((bf16[8,40,2048]{2,1,0:T(8,128)(2,1)}), bf16[8,40,2048]{2,1,0:T(8,128)(2,1)S(1)}, u32[]{:S(2)}, u32[]{:S(2)}) %all-to-all-start.6) | async-done | bytes 1310752 | tf_op jit(solution)/shard_map/all_to_all | solution.py:130
  337.0 7.2 %all-to-all-start.4 = ((bf16[8,40,2048]{2,1,0:T(8,128)(2,1)}), bf16[8,40,2048]{2,1,0:T(8,128)(2,1)S(1)}, u32[]{:S(2)}, u32[]{:S(2)}) async-start(bf16[8,40,2048]{2,1,0:T(8,128)(2,1)} %bitcast.71), calls=%async_computation.4 | async-start | bytes 2621440 | tf_op jit(solution)/shard_map/all_to_all | solution.py:92
  344.2 2.3 gather_fusion.1
  346.5 15.8 %all-to-all-done.4 = bf16[8,40,2048]{2,1,0:T(8,128)(2,1)S(1)} async-done(((bf16[8,40,2048]{2,1,0:T(8,128)(2,1)}), bf16[8,40,2048]{2,1,0:T(8,128)(2,1)S(1)}, u32[]{:S(2)}, u32[]{:S(2)}) %all-to-all-start.4) | async-done | bytes 1310752 | tf_op jit(solution)/shard_map/all_to_all | solution.py:92
  363.7 2.9 broadcast_select_fusion
  368.8 2.7 reshape.102
  372.7 4.7 reduce.1
  377.5 5.6 multiply_reduce_fusion.1
  383.1 45.0 %reduce-scatter.8.cloned.1.call-done = bf16[768,64]{0,1:T(8,128)(2,1)} async-done(((bf16[768,2048]{0,1:T(8,128)(2,1)}), bf16[768,64]{0,1:T(8,128)(2,1)}) %reduce-scatter.8.cloned.1.call-update) | async-done | bytes 98320 | tf_op jit(solution)/shard_map/reduce_scatter | solution.py:153
  429.7 124.2 %reduce-scatter.6.cloned.1.call-done = bf16[64,768]{1,0:T(8,128)(2,1)} async-done(((bf16[2048,768]{1,0:T(8,128)(2,1)}), bf16[64,768]{1,0:T(8,128)(2,1)}) %reduce-scatter.6.cloned.1.call-update) | async-done | bytes 98320 | tf_op jit(solution)/shard_map/reduce_scatter | solution.py:150
  555.5 124.2 %reduce-scatter.4.cloned.1.call-done = bf16[64,768]{1,0:T(8,128)(2,1)} async-done(((bf16[2048,768]{1,0:T(8,128)(2,1)}), bf16[64,768]{1,0:T(8,128)(2,1)}) %reduce-scatter.4.cloned.1.call-update) | async-done | bytes 98320 | tf_op jit(solution)/shard_map/reduce_scatter | solution.py:147
  (84 shorter events, 26.0 us)
Async XLA Ops:
  7.2 21.0 %copy-start = (bf16[1,768,2048]{2,1,0:T(8,128)(2,1)S(1)}, bf16[1,768,2048]{2,1,0:T(8,128)(2,1)}, u32[]{:S(2)}) copy-start(bf16[1,768,2048]{2,1,0:T(8,128)(2,1)} %param.17) | copy-start | bytes 9437188
  7.2 9.6 %copy-start.11 = (s32[8]{0:T(128)S(1)}, s32[8]{0:T(128)}, u32[]{:S(2)}) copy-start(s32[8]{0:T(128)} %param.14) | copy-start | bytes 100
  10.5 16.1 %all-to-all-start.2 = ((bf16[8,64,768]{2,1,0:T(8,128)(2,1)}), bf16[8,64,768]{2,1,0:T(8,128)(2,1)}, u32[]{:S(2)}, u32[]{:S(2)}) async-start(bf16[8,64,768]{2,1,0:T(8,128)(2,1)} %get-tuple-element.33), calls=%async_computation.2 | async-start | bytes 1572864 | tf_op jit(solution)/shard_map/all_to_all | solution.py:67
  16.8 107.7 %all-gather.9.cloned.1.call-start = ((), (), s32[]{:S(2)}) async-start(), calls=%async_computation.14 | async-start | bytes 3244032 | tf_op jit(solution)/shard_map/all_gather | solution.py:73
  28.2 178.8 %all-gather.11.cloned.1.call-start = ((), (), s32[]{:S(2)}) async-start(), calls=%async_computation.15 | async-start | bytes 3244032 | tf_op jit(solution)/shard_map/all_gather | solution.py:74
  28.4 16.4 %copy-start.6 = (bf16[8,64,768]{2,1,0:T(8,128)(2,1)S(1)}, bf16[8,64,768]{2,1,0:T(8,128)(2,1)}, u32[]{:S(2)}) copy-start(bf16[8,64,768]{2,1,0:T(8,128)(2,1)} %get-tuple-element.32) | copy-start | bytes 2359300
  28.5 30.8 %copy-start.9 = (s32[128,2]{0,1:T(2,128)S(1)}, s32[128,2]{0,1:T(2,128)}, u32[]{:S(2)}) copy-start(s32[128,2]{0,1:T(2,128)} %param.12) | copy-start | bytes 3076
  28.6 31.8 %copy-start.7 = (bf16[128,2048]{1,0:T(8,128)(2,1)S(1)}, bf16[128,2048]{1,0:T(8,128)(2,1)}, u32[]{:S(2)}) copy-start(bf16[128,2048]{1,0:T(8,128)(2,1)} %param.10) | copy-start | bytes 1572868
  44.7 245.3 %all-gather.7.cloned.1.call-start = ((), (), s32[]{:S(2)}) async-start(), calls=%async_computation.13 | async-start | bytes 3244032 | tf_op jit(solution)/shard_map/all_gather | solution.py:72
  61.7 7.8 %copy-start.8 = (bf16[128,2048]{1,0:T(8,128)(2,1)S(1)}, bf16[128,2048]{1,0:T(8,128)(2,1)}, u32[]{:S(2)}) copy-start(bf16[128,2048]{1,0:T(8,128)(2,1)} %param.11) | copy-start | bytes 1572868
  63.2 19.6 %all-to-all-start = ((bf16[8,40,2048]{2,1,0:T(8,128)(2,1)}), bf16[8,40,2048]{2,1,0:T(8,128)(2,1)}, u32[]{:S(2)}, u32[]{:S(2)}) async-start(bf16[8,40,2048]{2,1,0:T(8,128)(2,1)} %bitcast.3), calls=%async_computation | async-start | bytes 2621440 | tf_op jit(solution)/shard_map/all_to_all | solution.py:80
  71.9 2.7 copy-start.10
  74.6 8.2 %copy-start.2 = (f32[256,2048]{1,0:T(8,128)}, f32[256,2048]{1,0:T(8,128)S(1)}, u32[]{:S(2)}) copy-start(f32[256,2048]{1,0:T(8,128)S(1)} %mul.84) | copy-start | bytes 6291460
  82.8 45.1 %all-to-all-start.5 = ((bf16[8,40,2048]{2,1,0:T(8,128)(2,1)}), bf16[8,40,2048]{2,1,0:T(8,128)(2,1)}, u32[]{:S(2)}, u32[]{:S(2)}) async-start(bf16[8,40,2048]{2,1,0:T(8,128)(2,1)} %bitcast.70), calls=%async_computation.5 | async-start | bytes 2621440 | tf_op jit(solution)/shard_map/all_to_all | solution.py:115
  89.9 338.3 %reduce-scatter.8.cloned.1.call-start = ((), (), s32[]{:S(2)}) async-start(), calls=%async_computation.12 | async-start | bytes 3244032 | tf_op jit(solution)/shard_map/reduce_scatter | solution.py:153
  293.7 0.8 copy-start.15
  293.7 10.8 %copy-start.13 = (bf16[320,768]{1,0:T(8,128)(2,1)}, bf16[320,768]{1,0:T(8,128)(2,1)S(1)}, u32[]{:S(2)}) copy-start(bf16[320,768]{1,0:T(8,128)(2,1)S(1)} %get-tuple-element.27) | copy-start | bytes 1474564
  299.4 254.6 %reduce-scatter.6.cloned.1.call-start = ((), (), s32[]{:S(2)}) async-start(), calls=%async_computation.11 | async-start | bytes 3244032 | tf_op jit(solution)/shard_map/reduce_scatter | solution.py:150
  304.5 375.3 %reduce-scatter.4.cloned.1.call-start = ((), (), s32[]{:S(2)}) async-start(), calls=%async_computation.10 | async-start | bytes 3244032 | tf_op jit(solution)/shard_map/reduce_scatter | solution.py:147
  309.4 3.3 copy-start.12
  309.4 3.3 copy-start.14
  315.1 5.0 copy-start.16
  315.1 21.9 %all-to-all-start.6 = ((bf16[8,40,2048]{2,1,0:T(8,128)(2,1)}), bf16[8,40,2048]{2,1,0:T(8,128)(2,1)S(1)}, u32[]{:S(2)}, u32[]{:S(2)}) async-start(bf16[8,40,2048]{2,1,0:T(8,128)(2,1)} %bitcast.16), calls=%async_computation.6 | async-start | bytes 2621440 | tf_op jit(solution)/shard_map/all_to_all | solution.py:130
  337.0 25.4 %all-to-all-start.4 = ((bf16[8,40,2048]{2,1,0:T(8,128)(2,1)}), bf16[8,40,2048]{2,1,0:T(8,128)(2,1)S(1)}, u32[]{:S(2)}, u32[]{:S(2)}) async-start(bf16[8,40,2048]{2,1,0:T(8,128)(2,1)} %bitcast.71), calls=%async_computation.4 | async-start | bytes 2621440 | tf_op jit(solution)/shard_map/all_to_all | solution.py:92
  363.7 2.9 copy-start.4
  366.6 4.9 copy-start.5
  368.8 2.7 copy-start.3
  372.7 308.6 %copy-start.1 = (bf16[1,768,2048]{2,1,0:T(8,128)(2,1)S(1)}, bf16[1,768,2048]{2,1,0:T(8,128)(2,1)}, u32[]{:S(2)}) copy-start(bf16[1,768,2048]{2,1,0:T(8,128)(2,1)} %param.17) | copy-start | bytes 9437188
Sparse Core Ops, SparseCore 0:
  28.3 96.1 all-gather.8
  127.8 79.0 all-gather.10
  210.3 79.6 all-gather.6
  299.5 128.6 reduce-scatter.7
  432.2 121.7 reduce-scatter.5
  558.0 121.7 reduce-scatter.3
where the time goes:
time: 689 us; the launch traced here: 688 us
  waiting for transfers between devices  529 us (77%)
  matrix products  38.3 us (6%)
  starting transfers between devices  32.2 us (5%)
  blocking collectives  29.2 us (4%)
  local copies, waits for them, and re-layouts  21.9 us (3%)
  other arithmetic  21.5 us (3%)
  between operations  16.3 us (2%)
    reduce_scatter x1, waiting for transfers between devices, shards(): lax.psum_scatter(partial_gate.astype(jnp.bfloat16), 'dp', scatter_dimensi...  124 us
    reduce_scatter x1, waiting for transfers between devices, shards(): lax.psum_scatter(partial_up.astype(jnp.bfloat16), 'dp', scatter_dimension...  124 us
    all_gather x1, waiting for transfers between devices, shards(): lax.all_gather(mate_shares[0], 'dp', axis=0, tiled=True)  79.6 us
    all_gather x1, waiting for transfers between devices, shards(): lax.all_gather(mate_shares[2], 'dp', axis=1, tiled=True)  79 us
    reduce_scatter x1, waiting for transfers between devices, shards(): lax.psum_scatter(partial_down.astype(jnp.bfloat16), 'dp', scatter_dimensi...  45 us
    all_gather x1, waiting for transfers between devices, shards(): lax.all_gather(mate_shares[1], 'dp', axis=0, tiled=True)  34.6 us
    all_to_all x2, blocking collectives, shards(): lax.all_to_all(as_sent(outgoing), 'expert', split_axis=0, concat_axis=0,...  29.2 us
    all_to_all x1, waiting for transfers between devices, shards(): lax.all_to_all(expert_out.reshape(groups, capacity, model_width), 'expert...  15.8 us
  transfers between devices with their start and end apart: 11, of which 10 were waited for; matrix products, arithmetic and copies ran while one was open for 10% of the time, Pallas kernels for 0%

commit v1 on v0

--- a/solution.py
+++ b/solution.py
@@ -2,6 +2,11 @@
 import jax.numpy as jnp
 from jax import lax
 from jax.sharding import PartitionSpec as P
+
+
+def gather_over(x, axis, dim):
+    sent = jnp.stack([x] * lax.axis_size(axis))
+    return jnp.concatenate(lax.all_to_all(sent, axis, 0, 0), axis=dim)
 
 
 def as_sent(shard):
@@ -71,7 +76,7 @@
     gate_mat, up_mat, down_mat = (
         lax.all_gather(mate_shares[0], "dp", axis=0, tiled=True),
         lax.all_gather(mate_shares[1], "dp", axis=0, tiled=True),
-        lax.all_gather(mate_shares[2], "dp", axis=1, tiled=True),
+        gather_over(mate_shares[2], "dp", 1),
     )
     repeated = jnp.repeat(tokens, top_count, axis=0)
     outgoing_rows = jnp.dot(place_mat, repeated, preferred_element_type=jnp.float32).astype(

time: 689 us -> 625 us (0.907)
  waiting for transfers between devices: 529 us -> 467 us
  blocking collectives: 29.2 us -> 0 us
  starting transfers between devices: 32.2 us -> 55 us
    all_gather x1 -> x0, waiting for transfers between devices: 79 us -> none  [shards(): lax.all_gather(mate_shares[2], 'dp', axis=1, tiled=True)]
    all_to_all x0 -> x1, waiting for transfers between devices: none -> 75.4 us  [gather_over(): return jnp.concatenate(lax.all_to_all(sent, axis, 0, 0), axis=dim)]
    all_gather x1, waiting for transfers between devices: 79.6 us -> 21.5 us  [shards(): lax.all_gather(mate_shares[0], 'dp', axis=0, tiled=True)]
    all_gather x1, waiting for transfers between devices: 34.6 us -> 0.01 us  [shards(): lax.all_gather(mate_shares[1], 'dp', axis=0, tiled=True)]
    all_to_all x2 -> x0, blocking collectives: 29.2 us -> none  [shards(): lax.all_to_all(as_sent(outgoing), 'expert', split_axis=0, concat_axis=0,...]
    all_to_all x1, waiting for transfers between devices: 0.01 us -> 14.6 us  [shards(): lax.all_to_all(outgoing_grads.reshape(groups, capacity, model_width), 'ex...]
    all_to_all x0 -> x1, starting transfers between devices: none -> 13 us  [gather_over(): return jnp.concatenate(lax.all_to_all(sent, axis, 0, 0), axis=dim)]
    all_to_all x1 -> x3, starting transfers between devices: 6.32 us -> 18.2 us  [shards(): lax.all_to_all(as_sent(outgoing), 'expert', split_axis=0, concat_axis=0,...]
  transfers between devices with their start and end apart: 11 -> 13, of which waited for: 10 -> 12; matrix products, arithmetic and copies ran while one was open for 10% -> 11% of each run, Pallas kernels for 0% -> 0%
where the time goes in v1:
time: 625 us; the launch traced here: 624 us
  waiting for transfers between devices  467 us (75%)
  starting transfers between devices  55 us (9%)
  matrix products  37 us (6%)
  local copies, waits for them, and re-layouts  27.2 us (4%)
  other arithmetic  22 us (4%)
  between operations  15.9 us (3%)
    reduce_scatter x1, waiting for transfers between devices, shards(): lax.psum_scatter(partial_up.astype(jnp.bfloat16), 'dp', scatter_dimension...  124 us
    reduce_scatter x1, waiting for transfers between devices, shards(): lax.psum_scatter(partial_gate.astype(jnp.bfloat16), 'dp', scatter_dimensi...  124 us
    all_to_all x1, waiting for transfers between devices, gather_over(): return jnp.concatenate(lax.all_to_all(sent, axis, 0, 0), axis=dim)  75.4 us
    reduce_scatter x1, waiting for transfers between devices, shards(): lax.psum_scatter(partial_down.astype(jnp.bfloat16), 'dp', scatter_dimensi...  47 us
    all_gather x1, waiting for transfers between devices, shards(): lax.all_gather(mate_shares[0], 'dp', axis=0, tiled=True)  21.5 us
    all_to_all x3, starting transfers between devices, shards(): lax.all_to_all(as_sent(outgoing), 'expert', split_axis=0, concat_axis=0,...  18.2 us
    all_to_all x3, waiting for transfers between devices, shards(): lax.all_to_all(as_sent(outgoing), 'expert', split_axis=0, concat_axis=0,...  17.5 us
    all_to_all x1, waiting for transfers between devices, shards(): lax.all_to_all(outgoing_rows.reshape(groups, capacity, model_width), 'exp...  16.4 us
  transfers between devices with their start and end apart: 13, of which 12 were waited for; matrix products, arithmetic and copies ran while one was open for 11% of the time, Pallas kernels for 0%

profile of v1, /device:TPU:4, one launch (start us, length us, event | category | flops | bytes accessed | tf_op | source)
XLA Modules:
  0.0 624.1 jit_solution(12209930963555576033)
XLA Ops:
  10.5 6.3 %all-to-all-start.2 = ((bf16[8,64,768]{2,1,0:T(8,128)(2,1)}), bf16[8,64,768]{2,1,0:T(8,128)(2,1)}, u32[]{:S(2)}, u32[]{:S(2)}) async-start(bf16[8,64,768]{2,1,0:T(8,128)(2,1)} %get-tuple-element.27), calls=%async_computation.2 | async-start | bytes 1572864 | tf_op jit(solution)/shard_map/all_to_all | solution.py:72
  19.3 7.3 %all-to-all-done.2 = bf16[8,64,768]{2,1,0:T(8,128)(2,1)} async-done(((bf16[8,64,768]{2,1,0:T(8,128)(2,1)}), bf16[8,64,768]{2,1,0:T(8,128)(2,1)}, u32[]{:S(2)}, u32[]{:S(2)}) %all-to-all-start.2) | async-done | bytes 786464 | tf_op jit(solution)/shard_map/all_to_all | solution.py:72
  29.5 5.6 all-to-all-start.3
  36.0 8.6 %all-to-all-done.3 = bf16[8,768,64]{1,2,0:T(8,128)(2,1)S(1)} async-done(((bf16[8,768,64]{1,2,0:T(8,128)(2,1)}), bf16[8,768,64]{1,2,0:T(8,128)(2,1)S(1)}, u32[]{:S(2)}, u32[]{:S(2)}) %all-to-all-start.3) | async-done | bytes 786464 | tf_op jit(solution)/shard_map/all_to_all | solution.py:72
  44.7 6.3 %all-to-all-start.1 = ((bf16[8,64,768]{2,1,0:T(8,128)(2,1)}), bf16[8,64,768]{2,1,0:T(8,128)(2,1)}, u32[]{:S(2)}, u32[]{:S(2)}) async-start(bf16[8,64,768]{2,1,0:T(8,128)(2,1)} %get-tuple-element.26), calls=%async_computation.1 | async-start | bytes 1572864 | tf_op jit(solution)/shard_map/all_to_all | solution.py:72
  53.7 2.7 mul.84
  60.0 6.3 %all-to-all-start.6 = ((bf16[8,40,2048]{2,1,0:T(8,128)(2,1)}), bf16[8,40,2048]{2,1,0:T(8,128)(2,1)}, u32[]{:S(2)}, u32[]{:S(2)}) async-start(bf16[8,40,2048]{2,1,0:T(8,128)(2,1)} %bitcast.70), calls=%async_computation.6 | async-start | bytes 2621440 | tf_op jit(solution)/shard_map/all_to_all | solution.py:120
  66.3 14.6 %all-to-all-done.6 = bf16[8,40,2048]{2,1,0:T(8,128)(2,1)} async-done(((bf16[8,40,2048]{2,1,0:T(8,128)(2,1)}), bf16[8,40,2048]{2,1,0:T(8,128)(2,1)}, u32[]{:S(2)}, u32[]{:S(2)}) %all-to-all-start.6) | async-done | bytes 1310752 | tf_op jit(solution)/shard_map/all_to_all | solution.py:120
  83.0 13.0 %all-to-all-start.4 = ((bf16[32,768,64]{1,2,0:T(8,128)(2,1)}), bf16[32,768,64]{1,2,0:T(8,128)(2,1)}, u32[]{:S(2)}, u32[]{:S(2)}) async-start(bf16[32,768,64]{1,2,0:T(8,128)(2,1)} %stack.2), calls=%async_computation.4 | async-start | bytes 6291456 | tf_op jit(solution)/shard_map/all_to_all | solution.py:9
  100.4 75.4 %all-to-all-done.4 = bf16[32,768,64]{1,2,0:T(8,128)(2,1)} async-done(((bf16[32,768,64]{1,2,0:T(8,128)(2,1)}), bf16[32,768,64]{1,2,0:T(8,128)(2,1)}, u32[]{:S(2)}, u32[]{:S(2)}) %all-to-all-start.4) | async-done | bytes 3145760 | tf_op jit(solution)/shard_map/all_to_all | solution.py:9
  175.8 4.9 all-to-all-start
  180.7 3.5 fusion.20
  184.2 16.4 %all-to-all-done = bf16[8,40,2048]{2,1,0:T(8,128)(2,1)S(1)} async-done(((bf16[8,40,2048]{2,1,0:T(8,128)(2,1)}), bf16[8,40,2048]{2,1,0:T(8,128)(2,1)S(1)}, u32[]{:S(2)}, u32[]{:S(2)}) %all-to-all-start) | async-done | bytes 1310752 | tf_op jit(solution)/shard_map/all_to_all | solution.py:85
  200.6 4.0 fusion.2
  204.6 21.5 %all-gather.5.cloned.1.call-done = bf16[1,2048,768]{2,1,0:T(8,128)(2,1)} async-done(((bf16[1,64,768]{2,1,0:T(8,128)(2,1)}), bf16[1,2048,768]{2,1,0:T(8,128)(2,1)}) %all-gather.5.cloned.1.call-update) | async-done | bytes 3145744 | tf_op jit(solution)/shard_map/all_gather | solution.py:77
  226.1 4.4 multiply_convert_fusion.3
  231.3 4.8 convolution_convert_fusion
  236.4 3.5 convolution_convert_fusion.1
  240.9 3.5 convolution_convert_fusion.2
  245.5 4.3 convolution_convert_fusion.4
  249.8 5.0 all-to-all-start.5
  254.7 3.3 fusion
  260.4 11.3 %all-to-all-done.5 = bf16[8,40,2048]{2,1,0:T(8,128)(2,1)S(1)} async-done(((bf16[8,40,2048]{2,1,0:T(8,128)(2,1)}), bf16[8,40,2048]{2,1,0:T(8,128)(2,1)S(1)}, u32[]{:S(2)}, u32[]{:S(2)}) %all-to-all-start.5) | async-done | bytes 1310752 | tf_op jit(solution)/shard_map/all_to_all | solution.py:97
  271.7 7.2 %all-to-all-start.7 = ((bf16[8,40,2048]{2,1,0:T(8,128)(2,1)}), bf16[8,40,2048]{2,1,0:T(8,128)(2,1)S(1)}, u32[]{:S(2)}, u32[]{:S(2)}) async-start(bf16[8,40,2048]{2,1,0:T(8,128)(2,1)} %bitcast.75), calls=%async_computation.7 | async-start | bytes 2621440 | tf_op jit(solution)/shard_map/all_to_all | solution.py:135
  281.3 14.7 %all-to-all-done.7 = bf16[8,40,2048]{2,1,0:T(8,128)(2,1)S(1)} async-done(((bf16[8,40,2048]{2,1,0:T(8,128)(2,1)}), bf16[8,40,2048]{2,1,0:T(8,128)(2,1)S(1)}, u32[]{:S(2)}, u32[]{:S(2)}) %all-to-all-start.7) | async-done | bytes 1310752 | tf_op jit(solution)/shard_map/all_to_all | solution.py:135
  298.3 2.5 broadcast_select_fusion
  303.0 2.7 reshape.111
  306.9 4.7 reduce.1
  311.7 5.6 multiply_reduce_fusion.1
  317.3 47.0 %reduce-scatter.8.cloned.1.call-done = bf16[768,64]{0,1:T(8,128)(2,1)} async-done(((bf16[768,2048]{0,1:T(8,128)(2,1)}), bf16[768,64]{0,1:T(8,128)(2,1)}) %reduce-scatter.8.cloned.1.call-update) | async-done | bytes 98320 | tf_op jit(solution)/shard_map/reduce_scatter | solution.py:158
  365.9 124.3 %reduce-scatter.6.cloned.1.call-done = bf16[64,768]{1,0:T(8,128)(2,1)} async-done(((bf16[2048,768]{1,0:T(8,128)(2,1)}), bf16[64,768]{1,0:T(8,128)(2,1)}) %reduce-scatter.6.cloned.1.call-update) | async-done | bytes 98320 | tf_op jit(solution)/shard_map/reduce_scatter | solution.py:155
  491.8 124.2 %reduce-scatter.4.cloned.1.call-done = bf16[64,768]{1,0:T(8,128)(2,1)} async-done(((bf16[2048,768]{1,0:T(8,128)(2,1)}), bf16[64,768]{1,0:T(8,128)(2,1)}) %reduce-scatter.4.cloned.1.call-update) | async-done | bytes 98320 | tf_op jit(solution)/shard_map/reduce_scatter | solution.py:152
  (82 shorter events, 38.6 us)
Async XLA Ops:
  7.2 21.0 %copy-start = (bf16[1,768,2048]{2,1,0:T(8,128)(2,1)S(1)}, bf16[1,768,2048]{2,1,0:T(8,128)(2,1)}, u32[]{:S(2)}) copy-start(bf16[1,768,2048]{2,1,0:T(8,128)(2,1)} %param.17) | copy-start | bytes 9437188
  7.2 9.6 %copy-start.10 = (s32[8]{0:T(128)S(1)}, s32[8]{0:T(128)}, u32[]{:S(2)}) copy-start(s32[8]{0:T(128)} %param.14) | copy-start | bytes 100
  10.5 16.1 %all-to-all-start.2 = ((bf16[8,64,768]{2,1,0:T(8,128)(2,1)}), bf16[8,64,768]{2,1,0:T(8,128)(2,1)}, u32[]{:S(2)}, u32[]{:S(2)}) async-start(bf16[8,64,768]{2,1,0:T(8,128)(2,1)} %get-tuple-element.27), calls=%async_computation.2 | async-start | bytes 1572864 | tf_op jit(solution)/shard_map/all_to_all | solution.py:72
  16.8 18.3 %copy-start.8 = (s32[128,2]{0,1:T(2,128)S(1)}, s32[128,2]{0,1:T(2,128)}, u32[]{:S(2)}) copy-start(s32[128,2]{0,1:T(2,128)} %param.12) | copy-start | bytes 3076
  16.8 183.8 %all-gather.7.cloned.1.call-start = ((), (), s32[]{:S(2)}) async-start(), calls=%async_computation.15 | async-start | bytes 3244032 | tf_op jit(solution)/shard_map/all_gather | solution.py:78
  28.5 22.8 %copy-start.6 = (bf16[128,2048]{1,0:T(8,128)(2,1)S(1)}, bf16[128,2048]{1,0:T(8,128)(2,1)}, u32[]{:S(2)}) copy-start(bf16[128,2048]{1,0:T(8,128)(2,1)} %param.11) | copy-start | bytes 1572868
  29.5 15.2 %all-to-all-start.3 = ((bf16[8,768,64]{1,2,0:T(8,128)(2,1)}), bf16[8,768,64]{1,2,0:T(8,128)(2,1)S(1)}, u32[]{:S(2)}, u32[]{:S(2)}) async-start(bf16[8,768,64]{1,2,0:T(8,128)(2,1)} %broadcast_select_fusion.1), calls=%async_computation.3 | async-start | bytes 1572864 | tf_op jit(solution)/shard_map/all_to_all | solution.py:72
  44.7 15.3 %all-to-all-start.1 = ((bf16[8,64,768]{2,1,0:T(8,128)(2,1)}), bf16[8,64,768]{2,1,0:T(8,128)(2,1)}, u32[]{:S(2)}, u32[]{:S(2)}) async-start(bf16[8,64,768]{2,1,0:T(8,128)(2,1)} %get-tuple-element.26), calls=%async_computation.1 | async-start | bytes 1572864 | tf_op jit(solution)/shard_map/all_to_all | solution.py:72
  53.7 2.7 copy-start.9
  56.4 3.6 copy-start.2
  60.0 20.9 %all-to-all-start.6 = ((bf16[8,40,2048]{2,1,0:T(8,128)(2,1)}), bf16[8,40,2048]{2,1,0:T(8,128)(2,1)}, u32[]{:S(2)}, u32[]{:S(2)}) async-start(bf16[8,40,2048]{2,1,0:T(8,128)(2,1)} %bitcast.70), calls=%async_computation.6 | async-start | bytes 2621440 | tf_op jit(solution)/shard_map/all_to_all | solution.py:120
  83.0 14.6 %copy-start.7 = (bf16[128,2048]{1,0:T(8,128)(2,1)S(1)}, bf16[128,2048]{1,0:T(8,128)(2,1)}, u32[]{:S(2)}) copy-start(bf16[128,2048]{1,0:T(8,128)(2,1)} %param.10) | copy-start | bytes 1572868
  83.0 92.8 %all-to-all-start.4 = ((bf16[32,768,64]{1,2,0:T(8,128)(2,1)}), bf16[32,768,64]{1,2,0:T(8,128)(2,1)}, u32[]{:S(2)}, u32[]{:S(2)}) async-start(bf16[32,768,64]{1,2,0:T(8,128)(2,1)} %stack.2), calls=%async_computation.4 | async-start | bytes 6291456 | tf_op jit(solution)/shard_map/all_to_all | solution.py:9
  96.0 130.1 %all-gather.5.cloned.1.call-start = ((), (), s32[]{:S(2)}) async-start(), calls=%async_computation.14 | async-start | bytes 3244032 | tf_op jit(solution)/shard_map/all_gather | solution.py:77
  175.8 24.8 %all-to-all-start = ((bf16[8,40,2048]{2,1,0:T(8,128)(2,1)}), bf16[8,40,2048]{2,1,0:T(8,128)(2,1)S(1)}, u32[]{:S(2)}, u32[]{:S(2)}) async-start(bf16[8,40,2048]{2,1,0:T(8,128)(2,1)} %bitcast.3), calls=%async_computation | async-start | bytes 2621440 | tf_op jit(solution)/shard_map/all_to_all | solution.py:85
  180.7 183.6 %reduce-scatter.8.cloned.1.call-start = ((), (), s32[]{:S(2)}) async-start(), calls=%async_computation.13 | async-start | bytes 3244032 | tf_op jit(solution)/shard_map/reduce_scatter | solution.py:158
  230.5 0.8 copy-start.13
  236.1 254.1 %reduce-scatter.6.cloned.1.call-start = ((), (), s32[]{:S(2)}) async-start(), calls=%async_computation.12 | async-start | bytes 3244032 | tf_op jit(solution)/shard_map/reduce_scatter | solution.py:155
  239.8 1.0 copy-start.12
  239.9 376.1 %reduce-scatter.4.cloned.1.call-start = ((), (), s32[]{:S(2)}) async-start(), calls=%async_computation.11 | async-start | bytes 3244032 | tf_op jit(solution)/shard_map/reduce_scatter | solution.py:152
  244.4 1.1 copy-start.14
  249.8 21.9 %all-to-all-start.5 = ((bf16[8,40,2048]{2,1,0:T(8,128)(2,1)}), bf16[8,40,2048]{2,1,0:T(8,128)(2,1)S(1)}, u32[]{:S(2)}, u32[]{:S(2)}) async-start(bf16[8,40,2048]{2,1,0:T(8,128)(2,1)} %bitcast.14), calls=%async_computation.5 | async-start | bytes 2621440 | tf_op jit(solution)/shard_map/all_to_all | solution.py:97
  254.7 3.3 copy-start.11
  271.7 24.3 %all-to-all-start.7 = ((bf16[8,40,2048]{2,1,0:T(8,128)(2,1)}), bf16[8,40,2048]{2,1,0:T(8,128)(2,1)S(1)}, u32[]{:S(2)}, u32[]{:S(2)}) async-start(bf16[8,40,2048]{2,1,0:T(8,128)(2,1)} %bitcast.75), calls=%async_computation.7 | async-start | bytes 2621440 | tf_op jit(solution)/shard_map/all_to_all | solution.py:135
  296.0 2.3 copy-start.4
  300.8 4.9 copy-start.5
  303.0 2.7 copy-start.3
  306.9 310.6 %copy-start.1 = (bf16[1,768,2048]{2,1,0:T(8,128)(2,1)S(1)}, bf16[1,768,2048]{2,1,0:T(8,128)(2,1)}, u32[]{:S(2)}) copy-start(bf16[1,768,2048]{2,1,0:T(8,128)(2,1)} %param.17) | copy-start | bytes 9437188
Sparse Core Ops, SparseCore 0:
  28.3 94.7 all-gather.6
  126.5 99.5 all-gather.4
  236.2 128.0 reduce-scatter.7
  368.3 121.7 reduce-scatter.5
  494.2 121.7 reduce-scatter.3
